TPU v7x, 256 devices: a whole 4x4x8 slice. The times are simulated.
256 devices in a mesh: section: 2 (over x_hi), lat: 4 (over x_lo, core), lon: 32 (over y, z).
Axes of the slice: x: 4 (x_hi: 2, x_lo: 2; x = x_hi * 2 + x_lo), y: 4, z: 8, core: 2. Of those that a mesh axis runs over, the one named last changes fastest.
Arguments:
- window_input: bfloat16 [2, 16, 2176, 256], P(None, 'lat', 'lon'), may hold values from -8 to 8
- output_cotangent: bfloat16 [2, 16, 2176, 256], P(None, 'lat', 'lon'), may hold values from -6 to 6
- ocean_mask: int32 [16, 2176], P('lat', 'lon'), may hold values 0 or 1
- dw_kernel: bfloat16 [2, 49, 256], P('section'), may hold values from -1.5 to 1.5
- channel_params: bfloat16 [2, 5, 256], P('section'), may hold values from -1.5 to 1.5
- up_weight: bfloat16 [2, 256, 1024], P('section'), may hold values from -0.375 to 0.375
- up_bias: bfloat16 [2, 1024], P('section'), may hold values from -3 to 3
- down_weight: bfloat16 [2, 1024, 256], P('section'), may hold values from -0.1875 to 0.1875
Outputs:
- boundary: bfloat16 [2, 2, 16, 2176, 256], P('section', None, 'lat', 'lon')
- grad_kernel: float32 [2, 49, 256], P('section')
- grad_channels: float32 [2, 5, 256], P('section')
- grad_up: float32 [2, 256, 1024], P('section')
- grad_up_bias: float32 [2, 1024], P('section')
- grad_down: float32 [2, 1024, 256], P('section')
All inputs are finite; a program needn't handle non-finite values. No bound on the sum of `ocean_mask` on one device may be relied on, other than what follows from the above.
Results may differ from a plain program's by a relative error of at most 0.012.
Values may be sent and summed in bfloat16 or wider, within the bound.
A program may use at most 128 MiB of HBM per device.

v0:
```python
import math
import jax
import jax.numpy as jnp
from jax import lax
from jax.sharding import PartitionSpec as P

KERNEL = 7
ROWS_DEV = 4
COLS_DEV = 68
BATCH = 2
norm_eps = 1e-06
gelu_scale = 0.7978845608028654
gelu_cubic = 0.044715
rows_contract = (((0,), (0,)), ((), ()))
cols_contract = (((1,), (1,)), ((), ()))


def padded_2(block, sides, width, periodic):
    for axis, dim in sides:
        count = lax.axis_size(axis)
        forward = [(i, i + 1) for i in range(count - 1)]
        if periodic:
            forward.append((count - 1, 0))
        backward = [(target, source) for source, target in forward]
        low = lax.ppermute(
            lax.slice_in_dim(block, block.shape[dim] - width, None, axis=dim), axis, forward
        )
        high = lax.ppermute(lax.slice_in_dim(block, 0, width, axis=dim), axis, backward)
        block = jnp.concatenate([low, block, high], axis=dim)
    return block


def from_behind(value, axis, by):
    count = lax.axis_size(axis)
    pairs = [(i, i + by) for i in range(count) if 0 <= i + by < count]
    return lax.ppermute(value, axis, pairs)


def gelu_value(values):
    inner = gelu_scale * (values + gelu_cubic * values * values * values)
    return 0.5 * values * (1.0 + jnp.tanh(inner))


def gelu_slope(values):
    tangent = jnp.tanh(gelu_scale * (values + gelu_cubic * values * values * values))
    return 0.5 * (1.0 + tangent) + 0.5 * values * (1.0 - tangent * tangent) * gelu_scale * (
        1.0 + 3.0 * gelu_cubic * values * values
    )


def depthwise(padded, kernel, row_count, col_count):
    summed = jnp.zeros((padded.shape[0], row_count, col_count, padded.shape[3]), jnp.float32)
    for offset in range(KERNEL * KERNEL):
        row_off, col_off = divmod(offset, KERNEL)
        window = padded[:, row_off : row_off + row_count, col_off : col_off + col_count, :]
        summed = summed + window.astype(jnp.float32) * kernel[offset].astype(jnp.float32)
    return summed


def kernel_grads(padded, grad_conv, row_count, col_count):
    channels = grad_conv.shape[-1]
    grad_wide = grad_conv.astype(jnp.float32)
    tap_sums = []
    for offset in range(KERNEL * KERNEL):
        row_off, col_off = divmod(offset, KERNEL)
        window = padded[:, row_off : row_off + row_count, col_off : col_off + col_count, :].astype(
            jnp.float32
        )
        tap_sums.append(jnp.sum((grad_wide * window).reshape(-1, channels), axis=0))
    return (jnp.stack(tap_sums), jnp.sum(grad_wide.reshape(-1, channels), axis=0))


def cell_forward(conv_out, inputs, sea_mask, params, w_up, b_up, w_down):
    average = jnp.mean(conv_out, axis=-1, keepdims=True)
    centered = conv_out - average
    inverse = lax.rsqrt(jnp.mean(centered * centered, axis=-1, keepdims=True) + norm_eps)
    normed = centered * inverse
    scaled = (normed * params[1].astype(jnp.float32) + params[2].astype(jnp.float32)).astype(
        jnp.bfloat16
    )
    channels = scaled.shape[-1]
    flat_rows = scaled.reshape(-1, channels)
    hidden = jnp.dot(flat_rows, w_up, preferred_element_type=jnp.float32) + b_up.astype(jnp.float32)
    active = gelu_value(hidden).astype(jnp.bfloat16)
    branch = jnp.dot(active, w_down, preferred_element_type=jnp.float32) + params[3].astype(
        jnp.float32
    )
    branch = branch.reshape(conv_out.shape)
    output = (
        sea_mask * (inputs.astype(jnp.float32) + params[4].astype(jnp.float32) * branch)
    ).astype(jnp.bfloat16)
    return (output, (normed, inverse, flat_rows, hidden, active, branch))


def cell_backward(saved, sea_mask, cotangent, params, w_up, w_down):
    normed, inverse, flat_rows, hidden, active, branch = saved
    channels = normed.shape[-1]
    upstream = sea_mask * cotangent.astype(jnp.float32)
    grad_scale = jnp.sum((upstream * branch).reshape(-1, channels), axis=0)
    grad_branch = (
        (params[4].astype(jnp.float32) * upstream).astype(jnp.bfloat16).reshape(-1, channels)
    )
    grad_down = lax.dot_general(
        active, grad_branch, rows_contract, preferred_element_type=jnp.float32
    )
    grad_out_bias = jnp.sum(grad_branch.astype(jnp.float32), axis=0)
    grad_active = lax.dot_general(
        grad_branch, w_down, cols_contract, preferred_element_type=jnp.float32
    )
    grad_hidden = (grad_active * gelu_slope(hidden)).astype(jnp.bfloat16)
    grad_up = lax.dot_general(
        flat_rows, grad_hidden, rows_contract, preferred_element_type=jnp.float32
    )
    grad_up_bias = jnp.sum(grad_hidden.astype(jnp.float32), axis=0)
    grad_scaled = lax.dot_general(
        grad_hidden, w_up, cols_contract, preferred_element_type=jnp.float32
    )
    grad_scaled = grad_scaled.reshape(normed.shape)
    grad_gain = jnp.sum((grad_scaled * normed).reshape(-1, channels), axis=0)
    grad_shift = jnp.sum(grad_scaled.reshape(-1, channels), axis=0)
    grad_normed = grad_scaled * params[1].astype(jnp.float32)
    first_mean = jnp.mean(grad_normed, axis=-1, keepdims=True)
    second_mean = jnp.mean(grad_normed * normed, axis=-1, keepdims=True)
    grad_conv = (inverse * (grad_normed - first_mean - normed * second_mean)).astype(jnp.bfloat16)
    small = (grad_gain, grad_shift, grad_out_bias, grad_scale)
    return (grad_conv, upstream, small, grad_up, grad_up_bias, grad_down)


def halo_field(field):
    reach = KERNEL // 2
    beside_all = padded_2(field, (("lon", 2),), reach, True)
    return padded_2(beside_all, (("lat", 1),), reach, False)


def run_forward(field, sea_mask, weights):
    kernel, params, w_up, b_up, w_down = weights
    padded = halo_field(field)
    conv_out = depthwise(padded, kernel, field.shape[1], field.shape[2]) + params[0].astype(
        jnp.float32
    )
    output, saved = cell_forward(conv_out, field, sea_mask, params, w_up, b_up, w_down)
    return (output, (padded, saved))


def run_backward(stored, sea_mask, weights, cotangent):
    kernel, params, w_up, b_up, w_down = weights
    padded, saved = stored
    row_count, col_count = (cotangent.shape[1], cotangent.shape[2])
    grad_conv, upstream, small, grad_up, grad_bias, grad_down = cell_backward(
        saved, sea_mask, cotangent, params, w_up, w_down
    )
    tap_sums, bias_sum = kernel_grads(padded, grad_conv, row_count, col_count)
    spread = depthwise(halo_field(grad_conv), kernel[::-1], row_count, col_count)
    grad_input = (upstream + spread).astype(jnp.bfloat16)
    return (grad_input, (tap_sums, jnp.stack((bias_sum,) + small), grad_up, grad_bias, grad_down))


def on_device(
    window_input,
    output_cotangent,
    ocean_mask,
    dw_kernel,
    channel_params,
    up_weight,
    up_bias,
    down_weight,
):
    section = lax.axis_index("section")
    first_section = section == 0
    sea_mask = ocean_mask.astype(jnp.float32)[None, :, :, None]
    batch_size = window_input.shape[0]
    local = (dw_kernel[0], channel_params[0], up_weight[0], up_bias[0], down_weight[0])
    micro = 1
    size_micro = batch_size // micro
    zero_field = jnp.zeros((size_micro,) + window_input.shape[1:], jnp.bfloat16)
    received = zero_field
    stored = []
    outputs = []
    for tick in range(micro + 1):
        if tick < micro:
            own_part = window_input
        else:
            own_part = zero_field
        current = jnp.where(first_section, own_part, received)
        result, kept = run_forward(current, sea_mask, local)
        stored.append(kept)
        outputs.append(result)
        if tick < micro:
            received = from_behind(result, "section", 1)
    received = zero_field
    grad_inputs = []
    totals = None
    for tick in range(micro + 1):
        if tick < micro:
            own_part = output_cotangent
        else:
            own_part = zero_field
        current = jnp.where(first_section, received, own_part)
        kept = jax.tree.map(
            lambda before, behind: jnp.where(first_section, before, behind),
            stored[max(tick - 1, 0)],
            stored[min(tick + 1, micro)],
        )
        grad_input, grads = run_backward(kept, sea_mask, local, current)
        counted = jnp.where(
            first_section, 1.0 if tick >= 1 else 0.0, 1.0 if tick < micro else 0.0
        ).astype(jnp.float32)
        weighted = jax.tree.map(lambda member: member * counted, grads)
        if totals is None:
            totals = weighted
        else:
            totals = jax.tree.map(jnp.add, totals, weighted)
        grad_inputs.append(grad_input)
        if tick < micro:
            received = from_behind(grad_input, "section", -1)
    final = jnp.concatenate(outputs[1:], axis=0)
    starts = jnp.concatenate(grad_inputs[1:], axis=0)
    boundary = jnp.where(first_section, starts, final)[None]
    owned = tuple((member[None] for member in totals))
    summed = lax.psum((owned[0], owned[1], owned[2], owned[3], owned[4]), ("lat", "lon"))
    factor = 1.0 / math.sqrt(BATCH * ROWS_DEV * COLS_DEV)
    return (
        boundary,
        summed[0] * factor,
        summed[1] * factor,
        summed[2] * factor,
        summed[3] * factor,
        summed[4] * factor,
    )


def solution(mesh):
    in_specs = (
        P(None, "lat", "lon", None),
        P(None, "lat", "lon", None),
        P("lat", "lon"),
        P("section", None, None),
        P("section", None, None),
        P("section", None, None),
        P("section", None),
        P("section", None, None),
    )
    out_specs = (
        P("section", None, "lat", "lon", None),
        P("section", None, None),
        P("section", None, None),
        P("section", None, None),
        P("section", None),
        P("section", None, None),
    )
    return jax.shard_map(
        on_device, mesh=mesh, in_specs=in_specs, out_specs=out_specs, check_vma=False
    )
```

profile of v0, /device:TPU:4, one launch (start us, length us, event | category | flops | bytes accessed | tf_op | source)
XLA Modules:
  0.0 1807.4 jit_solution(11287534964740938511)
XLA Ops:
  8.4 8.4 collective-permute-start.1
  18.9 4.9 collective-permute-done
  28.0 2.1 collective-permute-done.3
  30.9 5.6 fusion.257
  38.1 3.1 fusion.4
  42.2 2.0 convolution_add_fusion.1
  48.2 8.8 collective-permute-done.4
  60.9 3.7 collective-permute-done.5
  65.6 3.9 collective-permute-start.7
  71.1 1.7 reshape.2386
  73.1 2.0 collective-permute-done.8
  76.1 5.6 fusion.255
  83.1 4.7 fusion.9
  91.4 2.2 multiply_reduce_fusion.3
  93.7 1.8 maximum_select_fusion
  98.3 1.8 fusion.146
  100.1 2.0 collective-permute-start.9
  103.8 3.3 collective-permute-done.9
  107.3 5.4 collective-permute-start.11
  114.2 1.9 convolution_add_fusion
  117.4 4.7 add_convert_fusion.1
  123.5 1.9 reshape.2391
  127.7 2.0 multiply_reduce_fusion.2
  129.8 2.8 convert_reduce_fusion.2
  132.6 1.9 fusion.254
  138.7 1.9 fusion.220
  143.4 1.7 collective-permute-start.14
  149.3 553.0 %all-reduce = (f32[1,49,256]{2,0,1:T(1,128)S(1)}, f32[1,5,256]{2,0,1:T(1,128)S(1)}, f32[1,1024]{1,0:T(1,128)S(1)}) all-reduce(f32[1,49,256]{2,0,1:T(1,128)S(1)} %multiply_add_fusion.3, f32[1,5,256]{2,0,1:T(1,128)S(1)} %multiply_add_fusion.4, f32[1,1024]{1,0:T(1,128)S(1)} %bitcast.416), channel_id=1, replica_groups=mesh['section'=2,'lat'=4,'lon'=32] {'lat','lon'}, use_global_device_ids=true, to_apply=%region_106.107 | all-reduce | flops 14848 | bytes 118784 | tf_op jit(solution)/shard_map/psum | solution.py:220
  707.4 4.9 collective-permute-done.17
  712.8 5.5 fusion.252
  719.1 1078.0 %all-reduce.4.cloned.1.call-done = (f32[1,256,1024]{2,1,0:T(8,128)}, f32[1,1024,256]{2,1,0:T(8,128)}) async-done(((f32[1,256,1024]{2,1,0:T(8,128)}, f32[1,1024,256]{2,1,0:T(8,128)}), (f32[1,256,1024]{2,1,0:T(8,128)}, f32[1,1024,256]{2,1,0:T(8,128)})) %all-reduce.4.cloned.1.call-update) | async-done | bytes 2097168 | tf_op jit(solution)/shard_map/psum | solution.py:220
  1797.0 2.4 broadcast_multiply_fusion.1
  (570 shorter events, 54.3 us)
Async XLA Ops:
  7.2 31.0 %copy-start = (bf16[1,256,1024]{2,1,0:T(8,128)(2,1)S(1)}, bf16[1,256,1024]{2,1,0:T(8,128)(2,1)}, u32[]{:S(2)}) copy-start(bf16[1,256,1024]{2,1,0:T(8,128)(2,1)} %param.13) | copy-start | bytes 1572868
  7.2 1789.8 %all-reduce.4.cloned.1.call-start = ((), (), s32[]{:S(2)}) async-start(), calls=%async_computation | async-start | bytes 4194304 | tf_op jit(solution)/shard_map/psum | solution.py:220
  7.2 19.3 %copy-start.173 = (bf16[1,5,256]{2,1,0:T(8,128)(2,1)S(1)}, bf16[1,5,256]{2,1,0:T(8,128)(2,1)}, u32[]{:S(2)}) copy-start(bf16[1,5,256]{2,1,0:T(8,128)(2,1)} %param.12) | copy-start | bytes 7684
  7.2 19.9 %copy-start.182 = (bf16[1,1024]{1,0:T(2,128)(2,1)S(1)}, bf16[1,1024]{1,0:T(2,128)(2,1)}, u32[]{:S(2)}) copy-start(bf16[1,1024]{1,0:T(2,128)(2,1)} %param.14) | copy-start | bytes 6148
  7.3 20.5 %copy-start.184 = (s32[4,68]{1,0:T(4,128)S(1)}, s32[4,68]{1,0:T(4,128)}, u32[]{:S(2)}) copy-start(s32[4,68]{1,0:T(4,128)} %param.10) | copy-start | bytes 3268
  7.3 20.5 %copy-start.32 = (bf16[1,49,256]{2,1,0:T(8,128)(2,1)S(1)}, bf16[1,49,256]{2,1,0:T(8,128)(2,1)}, u32[]{:S(2)}) copy-start(bf16[1,49,256]{2,1,0:T(8,128)(2,1)} %param.11) | copy-start | bytes 75268
  8.4 10.5 collective-permute-start.1
  16.8 7.1 collective-permute-start
  17.8 13.1 copy-start.39
  17.8 13.1 copy-start.42
  17.8 13.0 copy-start.45
  17.8 58.0 %copy-start.33 = (f32[1,1,256]{2,1,0:T(1,128)}, f32[1,1,256]{2,1,0:T(1,128)S(1)}, u32[]{:S(2)}) copy-start(f32[1,1,256]{2,1,0:T(1,128)S(1)} %get-tuple-element.177) | copy-start | bytes 3076
  17.8 58.0 %copy-start.35 = (f32[1,1,256]{2,1,0:T(1,128)}, f32[1,1,256]{2,1,0:T(1,128)S(1)}, u32[]{:S(2)}) copy-start(f32[1,1,256]{2,1,0:T(1,128)S(1)} %get-tuple-element.178) | copy-start | bytes 3076
  17.8 58.0 %copy-start.37 = (f32[1,1,256]{2,1,0:T(1,128)}, f32[1,1,256]{2,1,0:T(1,128)S(1)}, u32[]{:S(2)}) copy-start(f32[1,1,256]{2,1,0:T(1,128)S(1)} %get-tuple-element.179) | copy-start | bytes 3076
  24.0 4.0 collective-permute-start.2
  25.3 4.8 collective-permute-start.3
  45.3 36.4 %copy-start.4 = (f32[2,4,68,256]{3,2,1,0:T(8,128)}, f32[2,4,68,256]{3,2,1,0:T(8,128)S(1)}, u32[]{:S(2)}) copy-start(f32[2,4,68,256]{3,2,1,0:T(8,128)S(1)} %reshape.2385) | copy-start | bytes 1671172
  47.0 10.1 collective-permute-start.4
  57.1 3.8 collective-permute-start.6
  57.6 7.1 collective-permute-start.5
  65.6 7.5 collective-permute-start.7
  69.6 5.5 collective-permute-start.8
  100.1 14.1 copy-start.25
  100.1 3.7 collective-permute-start.10
  100.1 7.1 collective-permute-start.9
  107.3 9.2 collective-permute-start.11
  112.7 4.0 collective-permute-start.12
  122.2 5.5 collective-permute-start.13
  143.0 559.9 %collective-permute-start.15 = (bf16[2,4,3,256]{3,2,1,0:T(4,128)(2,1)S(1)}, bf16[2,4,3,256]{3,2,1,0:T(4,128)(2,1)S(1)}, u32[]{:S(2)}, u32[]{:S(2)}) collective-permute-start(bf16[2,4,3,256]{3,2,1,0:T(4,128)(2,1)S(1)} %get-tuple-element.158), channel_id=1, source_target_pairs={{1,0},{2,1},{3,2},{4,3},{5,4},{6,5},{7,6},{8,7},{9,8},{10,9},{11,1... | collective-permute-start | bytes 36872 | tf_op jit(solution)/shard_map/ppermute | solution.py:28
  143.4 559.5 %collective-permute-start.14 = (bf16[2,4,3,256]{3,2,1,0:T(4,128)(2,1)S(1)}, bf16[2,4,3,256]{3,2,1,0:T(4,128)(2,1)S(1)}, u32[]{:S(2)}, u32[]{:S(2)}) collective-permute-start(bf16[2,4,3,256]{3,2,1,0:T(4,128)(2,1)S(1)} %get-tuple-element.157), channel_id=1, source_target_pairs={{0,1},{1,2},{2,3},{3,4},{4,5},{5,6},{6,7},{7,8},{8,9},{9,10},{10,1... | collective-permute-start | bytes 36872 | tf_op jit(solution)/shard_map/ppermute | solution.py:25
  703.4 4.0 collective-permute-start.16
  704.8 7.5 collective-permute-start.17
  (174 other events, 837.8 us)
Sparse Core Ops, SparseCore 0:
  703.0 1093.9 all-reduce.3
where the time goes:
time: 1810 us
  waiting for transfers between devices  1110 us (61%)
  blocking collectives  553 us (31%)
  other arithmetic  51.6 us (3%)
  starting transfers between devices  34.9 us (2%)
  matrix products  23.5 us (1%)
    psum x1, waiting for transfers between devices, on_device(): lax.psum((owned[0], owned[1], owned[2], owned[3], owned[4]), ('lat', 'lon'))  1080 us
    psum x1, blocking collectives, on_device(): lax.psum((owned[0], owned[1], owned[2], owned[3], owned[4]), ('lat', 'lon'))  553 us
  transfers between devices with their start and end apart: 19, of which 12 were waited for; matrix products, arithmetic and copies ran while one was open for 1% of the time, Pallas kernels for 0%

commit v1 on v0

--- a/solution.py
+++ b/solution.py
@@ -217,7 +217,7 @@
     starts = jnp.concatenate(grad_inputs[1:], axis=0)
     boundary = jnp.where(first_section, starts, final)[None]
     owned = tuple((member[None] for member in totals))
-    summed = lax.psum((owned[0], owned[1], owned[2], owned[3], owned[4]), ("lat", "lon"))
+    summed = lax.psum(lax.psum((owned[0], owned[1], owned[2], owned[3], owned[4]), "lon"), "lat")
     factor = 1.0 / math.sqrt(BATCH * ROWS_DEV * COLS_DEV)
     return (
         boundary,

time: 1810 us -> 372 us (0.21)
  waiting for transfers between devices: 1110 us -> 79.7 us
  blocking collectives: 553 us -> 155 us
    psum x1 -> x2, waiting for transfers between devices: 1080 us -> 47.9 us  [the longest x1 47.8 us: on_device(): lax.psum(lax.psum((owned[0], owned[1], owned[2], owned[3], owned[4]), 'lo...]
    psum x1 -> x2, blocking collectives: 553 us -> 155 us  [the longest x1 141 us: on_device(): lax.psum((owned[0], owned[1], owned[2], owned[3], owned[4]), 'lon')]
  transfers between devices with their start and end apart: 19 -> 20, of which waited for: 12 -> 12; matrix products, arithmetic and copies ran while one was open for 1% -> 6% of each run, Pallas kernels for 0% -> 0%
where the time goes in v1:
time: 372 us; the launch traced here: 369 us
  blocking collectives  155 us (42%)
  waiting for transfers between devices  79.7 us (21%)
  other arithmetic  47.8 us (13%)
  starting transfers between devices  37.1 us (10%)
  matrix products  19.6 us (5%)
  between operations  16.5 us (4%)
  local copies, waits for them, and re-layouts  13.8 us (4%)
    psum x1, blocking collectives, on_device(): lax.psum((owned[0], owned[1], owned[2], owned[3], owned[4]), 'lon')  141 us
    psum x1, waiting for transfers between devices, on_device(): lax.psum(lax.psum((owned[0], owned[1], owned[2], owned[3], owned[4]), 'lo...  47.8 us
    ppermute x8, starting transfers between devices, padded_2(): lax.ppermute(lax.slice_in_dim(block, block.shape[dim] - width, None, axis...  19.2 us
    ppermute x8, starting transfers between devices, padded_2(): lax.ppermute(lax.slice_in_dim(block, 0, width, axis=dim), axis, backward)  14.4 us
    psum x1, blocking collectives, on_device(): lax.psum(lax.psum((owned[0], owned[1], owned[2], owned[3], owned[4]), 'lo...  13.4 us
    ppermute x8, waiting for transfers between devices, padded_2(): lax.ppermute(lax.slice_in_dim(block, block.shape[dim] - width, None, axis...  12 us
    ppermute x8, waiting for transfers between devices, padded_2(): lax.ppermute(lax.slice_in_dim(block, 0, width, axis=dim), axis, backward)  10.2 us
    reduce_sum x2, other arithmetic, cell_forward(): average = jnp.mean(conv_out, axis=-1, keepdims=True)  9.75 us
  transfers between devices with their start and end apart: 20, of which 12 were waited for; matrix products, arithmetic and copies ran while one was open for 6% of the time, Pallas kernels for 0%

profile of v1, /device:TPU:4, one launch (start us, length us, event | category | flops | bytes accessed | tf_op | source)
XLA Modules:
  0.0 369.3 jit_solution(6849069413259147806)
XLA Ops:
  8.4 8.4 %collective-permute-start.1 = (bf16[2,4,3,256]{3,2,1,0:T(4,128)(2,1)S(1)}, bf16[2,4,3,256]{3,2,1,0:T(4,128)(2,1)S(1)}, u32[]{:S(2)}, u32[]{:S(2)}) collective-permute-start(bf16[2,4,3,256]{3,2,1,0:T(4,128)(2,1)S(1)} %get-tuple-element.169), channel_id=1, source_target_pairs={{1,0},{2,1},{3,2},{4,3},{5,4},{6,5},{7,6},{8,7},{9,8},{10,9},{11,1... | collective-permute-start | bytes 36872 | tf_op jit(solution)/shard_map/ppermute | solution.py:28
  18.7 5.1 %collective-permute-done = bf16[2,4,3,256]{3,2,1,0:T(4,128)(2,1)S(1)} collective-permute-done((bf16[2,4,3,256]{3,2,1,0:T(4,128)(2,1)S(1)}, bf16[2,4,3,256]{3,2,1,0:T(4,128)(2,1)S(1)}, u32[]{:S(2)}, u32[]{:S(2)}) %collective-permute-start) | collective-permute-done | bytes 12320 | tf_op jit(solution)/shard_map/ppermute | solution.py:25
  28.0 2.1 collective-permute-done.3
  30.8 4.8 %fusion.257 = (f32[2,4,68]{2,1,0:T(4,128)S(1)}, f32[2,4,68,256]{3,2,1,0:T(8,128)S(1)}) fusion(f32[256]{0:T(256)S(1)} %bitcast.424, f32[256]{0:T(256)S(1)} %bitcast.332, bf16[2,7,74,256]{3,2,1,0:T(8,128)(2,1)S(1)} %get-tuple-element.157, f32[256]{0:T(256)S(1)} %bitcast.336, f32[256]{0:T(256)S(1)} %bitcast.224, f32[256]{0:T(256)S(1)} %bitcast.228, ...), kind=kLoop, calls=%fused_computation.622 | loop fusion | flops 23117280 | bytes 12611712 | tf_op jit(solution)/shard_map/reduce_sum | solution.py:74
  36.5 2.3 fusion.4
  42.4 8.8 %collective-permute-done.4 = bf16[2,4,68,256]{3,2,1,0:T(8,128)(2,1)S(1)} collective-permute-done((bf16[2,4,68,256]{3,2,1,0:T(8,128)(2,1)S(1)}, bf16[2,4,68,256]{3,2,1,0:T(8,128)(2,1)S(1)}, u32[]{:S(2)}, u32[]{:S(2)}) %collective-permute-start.4) | collective-permute-done | bytes 278560 | tf_op jit(solution)/shard_map/ppermute | solution.py:36
  51.6 1.8 collective-permute-start.5
  55.1 3.6 collective-permute-done.5
  59.5 4.0 %collective-permute-start.7 = (bf16[2,3,74,256]{3,2,1,0:T(8,128)(2,1)}, bf16[2,3,74,256]{3,2,1,0:T(8,128)(2,1)S(1)}, u32[]{:S(2)}, u32[]{:S(2)}) collective-permute-start(bf16[2,3,74,256]{3,2,1,0:T(8,128)(2,1)} %get-tuple-element.154), channel_id=1, source_target_pairs={{0,32},{32,64},{64,96},{1,33},{33,65},{65,97},{2,34},{34,66},{66,9... | collective-permute-start | bytes 681992 | tf_op jit(solution)/shard_map/ppermute | solution.py:25
  66.0 2.8 collective-permute-done.8
  69.7 4.9 %fusion.255 = (f32[2,4,68]{2,1,0:T(4,128)S(1)}, f32[2,4,68,256]{3,2,1,0:T(8,128)S(1)}) fusion(f32[256]{0:T(256)S(1)} %bitcast.425, f32[256]{0:T(256)S(1)} %bitcast.333, bf16[2,7,74,256]{3,2,1,0:T(8,128)(2,1)S(1)} %get-tuple-element.153, f32[256]{0:T(256)S(1)} %bitcast.337, f32[256]{0:T(256)S(1)} %bitcast.225, f32[256]{0:T(256)S(1)} %bitcast.229, ...), kind=kLoop, calls=%fused_computation.621 | loop fusion | flops 23117280 | bytes 12611712 | tf_op jit(solution)/shard_map/reduce_sum | solution.py:74
  75.3 4.7 %fusion.9 = (f32[544,1024]{1,0:T(8,128)S(1)}, bf16[544,1024]{1,0:T(8,128)(2,1)}) fusion(f32[544,1024]{1,0:T(8,128)} %get-tuple-element.229, f32[1024]{0:T(1024)S(1)} %bitcast.533, pred[]{:T(512)S(6)} %eq.3, bf16[544,256]{1,0:T(8,128)(2,1)S(1)} %reshape.2387, bf16[1,256,1024]{2,1,0:T(8,128)(2,1)S(1)} %copy-done), kind=kOutput, calls=%fused_computation.115 | convolution fusion | flops 301367296 | bytes 6377473 | tf_op jit(solution)/shard_map/dot_general | solution.py:83
  83.4 2.2 multiply_reduce_fusion.3
  85.8 1.9 maximum_select_fusion
  87.6 1.7 fusion.145
  90.4 1.9 fusion.146
  92.3 2.0 collective-permute-start.9
  96.0 3.3 collective-permute-done.9
  99.5 5.4 %collective-permute-start.11 = (bf16[2,3,74,256]{3,2,1,0:T(8,128)(2,1)S(1)}, bf16[2,3,74,256]{3,2,1,0:T(8,128)(2,1)S(1)}, u32[]{:S(2)}, u32[]{:S(2)}) collective-permute-start(bf16[2,3,74,256]{3,2,1,0:T(8,128)(2,1)S(1)} %get-tuple-element.150), channel_id=1, source_target_pairs={{0,32},{32,64},{64,96},{1,33},{33,65},{65,97},{2,34},{34,66},{66,9... | collective-permute-start | bytes 681992 | tf_op jit(solution)/shard_map/ppermute | solution.py:25
  109.1 5.4 %add_convert_fusion.1 = bf16[2,4,68,256]{3,2,1,0:T(8,128)(2,1)} fusion(bf16[2,4,68,256]{3,2,1,0:T(8,128)(2,1)S(1)} %get-tuple-element.135, bf16[2,4,3,256]{3,2,1,0:T(4,128)(2,1)S(1)} %collective-permute-done.10, bf16[2,4,3,256]{3,2,1,0:T(4,128)(2,1)S(1)} %collective-permute-done.9, bf16[2,7,74,256]{3,2,1,0:T(8,128)(2,1)S(1)} %get-tuple-element.149, ...), kind=kLoop, calls=%fused_computation.354 | loop fusion | flops 23535616 | bytes 12609601 | tf_op jit(solution)/shard_map/convert_element_type | solution.py:154
  114.5 2.1 collective-permute-start.13
  116.7 1.9 reshape.2391
  120.5 2.7 multiply_reduce_fusion.2
  124.2 2.8 convert_reduce_fusion.2
  135.2 2.0 collective-permute-start.14
  141.6 141.5 %all-reduce = (f32[1,49,256]{2,0,1:T(1,128)S(1)}, f32[1,5,256]{2,0,1:T(1,128)S(1)}, f32[1,1024]{1,0:T(1,128)S(1)}) all-reduce(f32[1,49,256]{2,0,1:T(1,128)S(1)} %multiply_add_fusion.3, f32[1,5,256]{2,0,1:T(1,128)S(1)} %multiply_add_fusion.4, f32[1,1024]{1,0:T(1,128)S(1)} %bitcast.419), channel_id=1, replica_groups=mesh['section'=2,'lat'=4,'lon'=32] {'lon'}, use_global_device_ids=true, to_apply=%region_106.107 | all-reduce | flops 14848 | bytes 118784 | tf_op jit(solution)/shard_map/psum | solution.py:220
  283.1 13.4 %all-reduce.2 = (f32[1,49,256]{2,0,1:T(1,128)S(1)}, f32[1,5,256]{2,0,1:T(1,128)S(1)}, f32[1,1024]{1,0:T(1,128)S(1)}) all-reduce(f32[1,49,256]{2,0,1:T(1,128)S(1)} %get-tuple-element.123, f32[1,5,256]{2,0,1:T(1,128)S(1)} %get-tuple-element.124, ...), channel_id=1, replica_groups=mesh['section'=2,'lat'=4,'lon'=32] {'lat'}, use_global_device_ids=true, to_apply=%region_107.108 | all-reduce | flops 14848 | bytes 118784 | tf_op jit(solution)/shard_map/psum | solution.py:220
  297.6 2.7 collective-permute-start.16
  302.8 2.1 collective-permute-done.17
  305.3 4.9 %fusion.252 = bf16[1,2,4,68,256]{4,3,2,1,0:T(8,128)(2,1)S(1)} fusion(f32[2,4,68,256]{3,2,1,0:T(8,128)S(1)} %copy-done.9, f32[256]{0:T(256)S(1)} %bitcast.418, f32[4,68]{1,0:T(4,128)S(1)} %convert_element_type.1601, f32[256]{0:T(256)S(1)} %bitcast.223, bf16[2,7,74,256]{3,2,1,0:T(8,128)(2,1)S(1)} %get-tuple-element.145, f32[256]{0:T(256)S(1)} %bitcast.343, ...), kind=kLoop, calls=%fused_computation.427 | loop fusion | flops 24510464 | bytes 13446209 | tf_op jit(solution)/shard_map/broadcast_in_dim | solution.py:218
  311.1 47.8 %all-reduce.9.cloned.1.call-done = (f32[1,256,1024]{2,1,0:T(8,128)}, f32[1,1024,256]{2,1,0:T(8,128)}) async-done(((f32[1,256,1024]{2,1,0:T(8,128)}, f32[1,1024,256]{2,1,0:T(8,128)}), (f32[1,256,1024]{2,1,0:T(8,128)}, f32[1,1024,256]{2,1,0:T(8,128)})) %all-reduce.9.cloned.1.call-update) | async-done | bytes 2097168 | tf_op jit(solution)/shard_map/psum | solution.py:220
  358.9 2.4 broadcast_multiply_fusion.1
  (488 shorter events, 49.2 us)
Async XLA Ops:
  7.2 29.3 %copy-start = (bf16[1,256,1024]{2,1,0:T(8,128)(2,1)S(1)}, bf16[1,256,1024]{2,1,0:T(8,128)(2,1)}, u32[]{:S(2)}) copy-start(bf16[1,256,1024]{2,1,0:T(8,128)(2,1)} %param.13) | copy-start | bytes 1572868
  7.2 290.0 %all-reduce.7.cloned.1.call-start = ((), (), s32[]{:S(2)}) async-start(), calls=%async_computation | async-start | bytes 4194304 | tf_op jit(solution)/shard_map/psum | solution.py:220
  7.2 19.4 %copy-start.131 = (bf16[1,5,256]{2,1,0:T(8,128)(2,1)S(1)}, bf16[1,5,256]{2,1,0:T(8,128)(2,1)}, u32[]{:S(2)}) copy-start(bf16[1,5,256]{2,1,0:T(8,128)(2,1)} %param.12) | copy-start | bytes 7684
  7.2 19.9 %copy-start.138 = (bf16[1,1024]{1,0:T(2,128)(2,1)S(1)}, bf16[1,1024]{1,0:T(2,128)(2,1)}, u32[]{:S(2)}) copy-start(bf16[1,1024]{1,0:T(2,128)(2,1)} %param.14) | copy-start | bytes 6148
  7.3 20.5 %copy-start.141 = (s32[4,68]{1,0:T(4,128)S(1)}, s32[4,68]{1,0:T(4,128)}, u32[]{:S(2)}) copy-start(s32[4,68]{1,0:T(4,128)} %param.10) | copy-start | bytes 3268
  7.3 20.5 %copy-start.37 = (bf16[1,49,256]{2,1,0:T(8,128)(2,1)S(1)}, bf16[1,49,256]{2,1,0:T(8,128)(2,1)}, u32[]{:S(2)}) copy-start(bf16[1,49,256]{2,1,0:T(8,128)(2,1)} %param.11) | copy-start | bytes 75268
  8.3 22.4 %copy-start.3 = (bf16[2,4,68,256]{3,2,1,0:T(8,128)(2,1)}, bf16[2,4,68,256]{3,2,1,0:T(8,128)(2,1)S(1)}, u32[]{:S(2)}) copy-start(bf16[2,4,68,256]{3,2,1,0:T(8,128)(2,1)S(1)} %copy_select_fusion) | copy-start | bytes 835588
  8.4 10.3 %collective-permute-start.1 = (bf16[2,4,3,256]{3,2,1,0:T(4,128)(2,1)S(1)}, bf16[2,4,3,256]{3,2,1,0:T(4,128)(2,1)S(1)}, u32[]{:S(2)}, u32[]{:S(2)}) collective-permute-start(bf16[2,4,3,256]{3,2,1,0:T(4,128)(2,1)S(1)} %get-tuple-element.169), channel_id=1, source_target_pairs={{1,0},{2,1},{3,2},{4,3},{5,4},{6,5},{7,6},{8,7},{9,8},{10,9},{11,1... | collective-permute-start | bytes 36872 | tf_op jit(solution)/shard_map/ppermute | solution.py:28
  16.8 7.1 %collective-permute-start = (bf16[2,4,3,256]{3,2,1,0:T(4,128)(2,1)S(1)}, bf16[2,4,3,256]{3,2,1,0:T(4,128)(2,1)S(1)}, u32[]{:S(2)}, u32[]{:S(2)}) collective-permute-start(bf16[2,4,3,256]{3,2,1,0:T(4,128)(2,1)S(1)} %get-tuple-element.168), channel_id=1, source_target_pairs={{0,1},{1,2},{2,3},{3,4},{4,5},{5,6},{6,7},{7,8},{8,9},{9,10},{10,1... | collective-permute-start | bytes 36872 | tf_op jit(solution)/shard_map/ppermute | solution.py:25
  18.7 50.7 %copy-start.38 = (f32[1,1,256]{2,1,0:T(1,128)}, f32[1,1,256]{2,1,0:T(1,128)S(1)}, u32[]{:S(2)}) copy-start(f32[1,1,256]{2,1,0:T(1,128)S(1)} %get-tuple-element.217) | copy-start | bytes 3076
  18.7 50.7 %copy-start.41 = (f32[1,1,256]{2,1,0:T(1,128)}, f32[1,1,256]{2,1,0:T(1,128)S(1)}, u32[]{:S(2)}) copy-start(f32[1,1,256]{2,1,0:T(1,128)S(1)} %get-tuple-element.218) | copy-start | bytes 3076
  24.0 4.0 %collective-permute-start.2 = (bf16[2,3,74,256]{3,2,1,0:T(8,128)(2,1)S(1)}, bf16[2,3,74,256]{3,2,1,0:T(8,128)(2,1)S(1)}, u32[]{:S(2)}, u32[]{:S(2)}) collective-permute-start(bf16[2,3,74,256]{3,2,1,0:T(8,128)(2,1)S(1)} %get-tuple-element.158), channel_id=1, source_target_pairs={{0,32},{32,64},{64,96},{1,33},{33,65},{65,97},{2,34},{34,66},{66,9... | collective-permute-start | bytes 681992 | tf_op jit(solution)/shard_map/ppermute | solution.py:25
  25.3 4.8 %collective-permute-start.3 = (bf16[2,3,74,256]{3,2,1,0:T(8,128)(2,1)S(1)}, bf16[2,3,74,256]{3,2,1,0:T(8,128)(2,1)S(1)}, u32[]{:S(2)}, u32[]{:S(2)}) collective-permute-start(bf16[2,3,74,256]{3,2,1,0:T(8,128)(2,1)S(1)} %get-tuple-element.159), channel_id=1, source_target_pairs={{32,0},{64,32},{96,64},{33,1},{65,33},{97,65},{34,2},{66,34},{98,6... | collective-permute-start | bytes 681992 | tf_op jit(solution)/shard_map/ppermute | solution.py:28
  28.0 41.5 %copy-start.44 = (f32[1,1,256]{2,1,0:T(1,128)}, f32[1,1,256]{2,1,0:T(1,128)S(1)}, u32[]{:S(2)}) copy-start(f32[1,1,256]{2,1,0:T(1,128)S(1)} %get-tuple-element.189) | copy-start | bytes 3076
  41.1 10.1 %collective-permute-start.4 = (bf16[2,4,68,256]{3,2,1,0:T(8,128)(2,1)S(1)}, bf16[2,4,68,256]{3,2,1,0:T(8,128)(2,1)S(1)}, u32[]{:S(2)}, u32[]{:S(2)}) collective-permute-start(bf16[2,4,68,256]{3,2,1,0:T(8,128)(2,1)S(1)} %get-tuple-element.227), channel_id=1, source_target_pairs={{0,128},{1,129},{2,130},{3,131},{4,132},{5,133},{6,134},{7,135},{8... | collective-permute-start | bytes 835592 | tf_op jit(solution)/shard_map/ppermute | solution.py:36
  51.2 23.4 %copy-start.5 = (bf16[2,4,68,256]{3,2,1,0:T(8,128)(2,1)}, bf16[2,4,68,256]{3,2,1,0:T(8,128)(2,1)S(1)}, u32[]{:S(2)}) copy-start(bf16[2,4,68,256]{3,2,1,0:T(8,128)(2,1)S(1)} %broadcast_select_fusion.5) | copy-start | bytes 835588
  51.3 3.8 %collective-permute-start.6 = (bf16[2,4,3,256]{3,2,1,0:T(4,128)(2,1)S(1)}, bf16[2,4,3,256]{3,2,1,0:T(4,128)(2,1)S(1)}, u32[]{:S(2)}, u32[]{:S(2)}) collective-permute-start(bf16[2,4,3,256]{3,2,1,0:T(4,128)(2,1)S(1)} %get-tuple-element.167), channel_id=1, source_target_pairs={{1,0},{2,1},{3,2},{4,3},{5,4},{6,5},{7,6},{8,7},{9,8},{10,9},{11,1... | collective-permute-start | bytes 36872 | tf_op jit(solution)/shard_map/ppermute | solution.py:28
  51.6 7.1 %collective-permute-start.5 = (bf16[2,4,3,256]{3,2,1,0:T(4,128)(2,1)S(1)}, bf16[2,4,3,256]{3,2,1,0:T(4,128)(2,1)S(1)}, u32[]{:S(2)}, u32[]{:S(2)}) collective-permute-start(bf16[2,4,3,256]{3,2,1,0:T(4,128)(2,1)S(1)} %get-tuple-element.166), channel_id=1, source_target_pairs={{0,1},{1,2},{2,3},{3,4},{4,5},{5,6},{6,7},{7,8},{8,9},{9,10},{10,1... | collective-permute-start | bytes 36872 | tf_op jit(solution)/shard_map/ppermute | solution.py:25
  59.5 6.5 %collective-permute-start.7 = (bf16[2,3,74,256]{3,2,1,0:T(8,128)(2,1)}, bf16[2,3,74,256]{3,2,1,0:T(8,128)(2,1)S(1)}, u32[]{:S(2)}, u32[]{:S(2)}) collective-permute-start(bf16[2,3,74,256]{3,2,1,0:T(8,128)(2,1)} %get-tuple-element.154), channel_id=1, source_target_pairs={{0,32},{32,64},{64,96},{1,33},{33,65},{65,97},{2,34},{34,66},{66,9... | collective-permute-start | bytes 681992 | tf_op jit(solution)/shard_map/ppermute | solution.py:25
  63.5 5.2 %collective-permute-start.8 = (bf16[2,3,74,256]{3,2,1,0:T(8,128)(2,1)S(1)}, bf16[2,3,74,256]{3,2,1,0:T(8,128)(2,1)S(1)}, u32[]{:S(2)}, u32[]{:S(2)}) collective-permute-start(bf16[2,3,74,256]{3,2,1,0:T(8,128)(2,1)S(1)} %get-tuple-element.155), channel_id=1, source_target_pairs={{32,0},{64,32},{96,64},{33,1},{65,33},{97,65},{34,2},{66,34},{98,6... | collective-permute-start | bytes 681992 | tf_op jit(solution)/shard_map/ppermute | solution.py:28
  92.3 14.1 %copy-start.30 = (bf16[544,1024]{1,0:T(8,128)(2,1)S(1)}, bf16[544,1024]{1,0:T(8,128)(2,1)}, u32[]{:S(2)}) copy-start(bf16[544,1024]{1,0:T(8,128)(2,1)} %get-tuple-element.143) | copy-start | bytes 3342340
  92.3 14.1 %copy-start.125 = (f32[1,1,256]{2,1,0:T(1,128)S(1)}, f32[1,1,256]{2,1,0:T(1,128)}, u32[]{:S(2)}) copy-start(f32[1,1,256]{2,1,0:T(1,128)} %get-tuple-element.224) | copy-start | bytes 3076
  92.3 3.7 %collective-permute-start.10 = (bf16[2,4,3,256]{3,2,1,0:T(4,128)(2,1)S(1)}, bf16[2,4,3,256]{3,2,1,0:T(4,128)(2,1)S(1)}, u32[]{:S(2)}, u32[]{:S(2)}) collective-permute-start(bf16[2,4,3,256]{3,2,1,0:T(4,128)(2,1)S(1)} %get-tuple-element.165), channel_id=1, source_target_pairs={{1,0},{2,1},{3,2},{4,3},{5,4},{6,5},{7,6},{8,7},{9,8},{10,9},{11,1... | collective-permute-start | bytes 36872 | tf_op jit(solution)/shard_map/ppermute | solution.py:28
  92.3 7.1 %collective-permute-start.9 = (bf16[2,4,3,256]{3,2,1,0:T(4,128)(2,1)S(1)}, bf16[2,4,3,256]{3,2,1,0:T(4,128)(2,1)S(1)}, u32[]{:S(2)}, u32[]{:S(2)}) collective-permute-start(bf16[2,4,3,256]{3,2,1,0:T(4,128)(2,1)S(1)} %get-tuple-element.164), channel_id=1, source_target_pairs={{0,1},{1,2},{2,3},{3,4},{4,5},{5,6},{6,7},{7,8},{8,9},{9,10},{10,1... | collective-permute-start | bytes 36872 | tf_op jit(solution)/shard_map/ppermute | solution.py:25
  99.5 8.4 %collective-permute-start.11 = (bf16[2,3,74,256]{3,2,1,0:T(8,128)(2,1)S(1)}, bf16[2,3,74,256]{3,2,1,0:T(8,128)(2,1)S(1)}, u32[]{:S(2)}, u32[]{:S(2)}) collective-permute-start(bf16[2,3,74,256]{3,2,1,0:T(8,128)(2,1)S(1)} %get-tuple-element.150), channel_id=1, source_target_pairs={{0,32},{32,64},{64,96},{1,33},{33,65},{65,97},{2,34},{34,66},{66,9... | collective-permute-start | bytes 681992 | tf_op jit(solution)/shard_map/ppermute | solution.py:25
  104.9 3.9 %collective-permute-start.12 = (bf16[2,3,74,256]{3,2,1,0:T(8,128)(2,1)S(1)}, bf16[2,3,74,256]{3,2,1,0:T(8,128)(2,1)S(1)}, u32[]{:S(2)}, u32[]{:S(2)}) collective-permute-start(bf16[2,3,74,256]{3,2,1,0:T(8,128)(2,1)S(1)} %get-tuple-element.151), channel_id=1, source_target_pairs={{32,0},{64,32},{96,64},{33,1},{65,33},{97,65},{34,2},{66,34},{98,6... | collective-permute-start | bytes 681992 | tf_op jit(solution)/shard_map/ppermute | solution.py:28
  114.5 6.0 %collective-permute-start.13 = (bf16[2,4,68,256]{3,2,1,0:T(8,128)(2,1)}, bf16[2,4,68,256]{3,2,1,0:T(8,128)(2,1)}, u32[]{:S(2)}, u32[]{:S(2)}) collective-permute-start(bf16[2,4,68,256]{3,2,1,0:T(8,128)(2,1)} %add_convert_fusion.1), channel_id=1, source_target_pairs={{128,0},{129,1},{130,2},{131,3},{132,4},{133,5},{134,6},{135,7},{1... | collective-permute-start | bytes 835592 | tf_op jit(solution)/shard_map/ppermute | solution.py:36
  135.1 162.0 %collective-permute-start.15 = (bf16[2,4,3,256]{3,2,1,0:T(4,128)(2,1)S(1)}, bf16[2,4,3,256]{3,2,1,0:T(4,128)(2,1)S(1)}, u32[]{:S(2)}, u32[]{:S(2)}) collective-permute-start(bf16[2,4,3,256]{3,2,1,0:T(4,128)(2,1)S(1)} %get-tuple-element.163), channel_id=1, source_target_pairs={{1,0},{2,1},{3,2},{4,3},{5,4},{6,5},{7,6},{8,7},{9,8},{10,9},{11,1... | collective-permute-start | bytes 36872 | tf_op jit(solution)/shard_map/ppermute | solution.py:28
  135.2 161.9 %collective-permute-start.14 = (bf16[2,4,3,256]{3,2,1,0:T(4,128)(2,1)S(1)}, bf16[2,4,3,256]{3,2,1,0:T(4,128)(2,1)S(1)}, u32[]{:S(2)}, u32[]{:S(2)}) collective-permute-start(bf16[2,4,3,256]{3,2,1,0:T(4,128)(2,1)S(1)} %get-tuple-element.162), channel_id=1, source_target_pairs={{0,1},{1,2},{2,3},{3,4},{4,5},{5,6},{6,7},{7,8},{8,9},{9,10},{10,1... | collective-permute-start | bytes 36872 | tf_op jit(solution)/shard_map/ppermute | solution.py:25
  141.1 217.8 %all-reduce.9.cloned.1.call-start = ((), (), s32[]{:S(2)}) async-start(), calls=%async_computation.1 | async-start | bytes 4194304 | tf_op jit(solution)/shard_map/psum | solution.py:220
  297.6 5.2 %collective-permute-start.16 = (bf16[2,3,74,256]{3,2,1,0:T(8,128)(2,1)S(1)}, bf16[2,3,74,256]{3,2,1,0:T(8,128)(2,1)S(1)}, u32[]{:S(2)}, u32[]{:S(2)}) collective-permute-start(bf16[2,3,74,256]{3,2,1,0:T(8,128)(2,1)S(1)} %get-tuple-element.146), channel_id=1, source_target_pairs={{0,32},{32,64},{64,96},{1,33},{33,65},{65,97},{2,34},{34,66},{66,9... | collective-permute-start | bytes 681992 | tf_op jit(solution)/shard_map/ppermute | solution.py:25
  300.2 4.7 %collective-permute-start.17 = (bf16[2,3,74,256]{3,2,1,0:T(8,128)(2,1)S(1)}, bf16[2,3,74,256]{3,2,1,0:T(8,128)(2,1)S(1)}, u32[]{:S(2)}, u32[]{:S(2)}) collective-permute-start(bf16[2,3,74,256]{3,2,1,0:T(8,128)(2,1)S(1)} %get-tuple-element.147), channel_id=1, source_target_pairs={{32,0},{64,32},{96,64},{33,1},{65,33},{97,65},{34,2},{66,34},{98,6... | collective-permute-start | bytes 681992 | tf_op jit(solution)/shard_map/ppermute | solution.py:28
  (132 other events, 560.7 us)
Sparse Core Ops, SparseCore 0:
  141.2 155.0 all-reduce.6
  299.2 59.6 all-reduce.8
